TPU v7x, 256 devices: a whole 4x4x8 slice. The times are simulated.
256 devices in a mesh: dp: 4 (over y), tensor: 16 (over x_hi, z), rep: 4 (over x_lo, core).
Axes of the slice: x: 4 (x_hi: 2, x_lo: 2; x = x_hi * 2 + x_lo), y: 4, z: 8, core: 2. Of those that a mesh axis runs over, the one named last changes fastest.
Arguments:
- resid: bfloat16 [512, 8192], P('dp', 'rep'), may hold values from -94 to 94
- norm_gain: float32 [8192], P('rep'), may hold values from 0.25 to 1.75
- gate_weight: bfloat16 [4, 2048, 14336], P('rep', 'dp', 'tensor'), may hold values from -0.0625 to 0.0625
- up_weight: bfloat16 [4, 2048, 14336], P('rep', 'dp', 'tensor'), may hold values from -0.0625 to 0.0625
- down_weight: bfloat16 [14336, 4, 2048], P('tensor', 'rep', 'dp'), may hold values from -0.046875 to 0.046875
- enc_weight: bfloat16 [8192, 65536], P('rep', ('dp', 'tensor')), may hold values from -0.0625 to 0.0625
- enc_bias: float32 [65536], P(('dp', 'tensor')), may hold values from -3 to 3
- dec_weight: bfloat16 [65536, 8192], P(('dp', 'tensor'), 'rep'), may hold values from -1 to 1
- dec_bias: float32 [8192], P('rep'), may hold values from -3 to 3
- latent_ids: int32 [512, 64], replicated, may hold values from 0 to 65535, as said below
Outputs:
- resid_out: bfloat16 [512, 8192], P(('dp', 'tensor'), 'rep')
- recon: bfloat16 [512, 8192], P(('dp', 'tensor'), 'rep')
- error_ratio: float32 [512], P(('dp', 'tensor'))
Inputs may be any that keep to these rules, and one draw needn't show every extreme that they name: `latent_ids`: each row names 64 distinct latents: 8 latents in each of 8 distinct blocks of 128 consecutive latents (block b holds latents b * 128 to b * 128 + 127).
All inputs are finite; a program needn't handle non-finite values.
Results may differ from a plain program's by a relative error of at most 0.009.
Values may be sent and summed in bfloat16 or wider, within the bound.
No kernel may reach another device: no remote copies, remote signals or barrier semaphores. Data moves between devices by JAX's collectives and lax.ppermute only.
A program may use at most 64 MiB of HBM per device.

v0:
```python
import jax
import jax.numpy as jnp
from jax import lax
from jax.sharding import PartitionSpec as P


def place_mask(latent_ids, length, slab_first, slab_width):
    slots = latent_ids - slab_first
    inside = (slots >= 0) & (slots < slab_width)
    local_slot = jnp.where(inside, slots, slab_width)
    row_number = lax.broadcasted_iota(jnp.int32, slots.shape, 0)
    return (
        jnp.zeros((length, slab_width), jnp.bool_).at[row_number, local_slot].set(True, mode="drop")
    )


def body(
    resid,
    norm_gain,
    gate_weight,
    up_weight,
    down_weight,
    enc_weight,
    enc_bias,
    dec_weight,
    dec_bias,
    latent_ids,
):
    tok_grp, width_rep = resid.shape
    n_tensor = lax.axis_size("tensor")
    n_rep = lax.axis_size("rep")
    resid_f = resid.astype(jnp.float32)
    squares = lax.psum(jnp.sum(resid_f * resid_f, axis=1), "rep")
    inverse_rms = lax.rsqrt(squares / (width_rep * n_rep) + 1e-05)
    normed = (resid_f * inverse_rms[:, None] * norm_gain[None, :]).astype(jnp.bfloat16)
    gate_part = jnp.dot(
        normed,
        lax.all_gather(gate_weight, "dp", axis=1, tiled=True)[0],
        preferred_element_type=jnp.float32,
    )
    up_part = jnp.dot(
        normed,
        lax.all_gather(up_weight, "dp", axis=1, tiled=True)[0],
        preferred_element_type=jnp.float32,
    )
    gate_pre, up_pre = lax.psum((gate_part, up_part), "rep")
    hidden = (jax.nn.silu(gate_pre) * up_pre).astype(jnp.bfloat16)
    down_terms = jnp.dot(
        hidden,
        lax.all_gather(down_weight, "dp", axis=2, tiled=True)[:, 0, :],
        preferred_element_type=jnp.float32,
    )
    rows_dev = tok_grp // n_tensor
    block_sum = lax.psum(down_terms, "tensor")
    group_out = (resid_f + block_sum).astype(jnp.bfloat16)
    resid_rows = lax.dynamic_slice_in_dim(
        group_out, lax.axis_index("tensor") * rows_dev, rows_dev, 0
    )
    slab_input = lax.all_gather(group_out, "dp", axis=0, tiled=True)
    slab_width = enc_weight.shape[1]
    centred = (slab_input.astype(jnp.float32) - dec_bias[None, :]).astype(jnp.bfloat16)
    slab_first = (lax.axis_index("dp") * n_tensor + lax.axis_index("tensor")) * slab_width
    preact = lax.psum(jnp.dot(centred, enc_weight, preferred_element_type=jnp.float32), "rep")
    length = preact.shape[0]
    chosen = place_mask(latent_ids, length, slab_first, slab_width)
    actives = jnp.where(chosen, jnp.maximum(preact + enc_bias[None, :], 0.0), 0.0).astype(
        jnp.bfloat16
    )
    decoded = (
        lax.psum_scatter(
            jnp.dot(actives, dec_weight, preferred_element_type=jnp.float32),
            ("dp", "tensor"),
            scatter_dimension=0,
            tiled=True,
        )
        + dec_bias[None, :]
    )
    kept_f = resid_rows.astype(jnp.float32)
    misfit = kept_f - decoded
    miss_sum, energy = lax.psum(
        (jnp.sum(misfit * misfit, axis=1), jnp.sum(kept_f * kept_f, axis=1)), "rep"
    )
    error_ratio = miss_sum / (energy + 1e-06)
    return (resid_rows, decoded.astype(jnp.bfloat16), error_ratio)


def solution(mesh):
    in_specs = (
        P("dp", "rep"),
        P("rep"),
        P("rep", "dp", "tensor"),
        P("rep", "dp", "tensor"),
        P("tensor", "rep", "dp"),
        P("rep", ("dp", "tensor")),
        P(("dp", "tensor")),
        P(("dp", "tensor"), "rep"),
        P("rep"),
        P(),
    )
    out_specs = (P(("dp", "tensor"), "rep"), P(("dp", "tensor"), "rep"), P(("dp", "tensor")))
    return jax.shard_map(body, mesh=mesh, in_specs=in_specs, out_specs=out_specs, check_vma=False)
```

profile of v0, /device:TPU:1, one launch (start us, length us, event | category | flops | bytes accessed | tf_op | source)
XLA Modules:
  0.0 939.6 jit_solution(7741894260135573512)
XLA Ops:
  7.2 0.7 all-gather.7.cloned.1.call-update
  8.0 0.7 all-gather.5.cloned.1.call-update
  8.7 0.7 all-gather.9.cloned.1.call-update
  9.5 1.2 fusion.8
  10.7 8.3 psum.49
  18.9 41.2 %all-gather.7.cloned.1.call-done = bf16[1,2048,896]{2,1,0:T(8,128)(2,1)} async-done(((bf16[1,512,896]{2,1,0:T(8,128)(2,1)}), bf16[1,2048,896]{2,1,0:T(8,128)(2,1)}) %all-gather.7.cloned.1.call-update) | async-done | bytes 3670032 | tf_op jit(solution)/shard_map/all_gather | solution.py:43
  60.1 3.8 fusion.2
  63.9 44.8 %all-gather.5.cloned.1.call-done = bf16[1,2048,896]{2,1,0:T(8,128)(2,1)} async-done(((bf16[1,512,896]{2,1,0:T(8,128)(2,1)}), bf16[1,2048,896]{2,1,0:T(8,128)(2,1)}) %all-gather.5.cloned.1.call-update) | async-done | bytes 3670032 | tf_op jit(solution)/shard_map/all_gather | solution.py:38
  108.7 3.6 fusion.4
  112.4 44.9 %all-gather.9.cloned.1.call-done = bf16[896,1,2048]{2,0,1:T(8,128)(2,1)} async-done(((bf16[896,1,512]{2,0,1:T(8,128)(2,1)}), bf16[896,1,2048]{2,0,1:T(8,128)(2,1)}) %all-gather.9.cloned.1.call-update) | async-done | bytes 3670032 | tf_op jit(solution)/shard_map/all_gather | solution.py:50
  157.3 48.5 %all-reduce.10.cloned.1.call-done = (f32[128,896]{1,0:T(8,128)}, f32[128,896]{1,0:T(8,128)}) async-done(((f32[128,896]{1,0:T(8,128)}, f32[128,896]{1,0:T(8,128)}), (f32[128,896]{1,0:T(8,128)}, f32[128,896]{1,0:T(8,128)})) %all-reduce.10.cloned.1.call-update) | async-done | bytes 917520 | tf_op jit(solution)/shard_map/psum | solution.py:46
  205.8 4.0 fusion
  210.0 149.3 %all-reduce.6.cloned.1.call-done = f32[128,2048]{1,0:T(8,128)} async-done(((f32[128,2048]{1,0:T(8,128)}), f32[128,2048]{1,0:T(8,128)}) %all-reduce.6.cloned.1.call-update) | async-done | bytes 1048592 | tf_op jit(solution)/shard_map/psum | solution.py:54
  359.2 2.1 fusion.11
  361.5 41.0 %all-gather.11.cloned.1.call-done = bf16[512,2048]{1,0:T(8,128)(2,1)} async-done(((bf16[128,2048]{1,0:T(8,128)(2,1)}), bf16[512,2048]{1,0:T(8,128)(2,1)}) %all-gather.11.cloned.1.call-update) | async-done | bytes 2097168 | tf_op jit(solution)/shard_map/all_gather | solution.py:59
  402.4 6.5 fusion.6
  409.4 0.1 copy.13
  409.6 137.1 %scatter_custom_fusion = pred[524288]{0:T(1024)(128)(4,1)S(1)} fusion(s32[32768]{0:T(1024)S(1)} %reshape.26, pred[32768]{0:T(1024)(128)(4,1)S(1)} %broadcast.49, pred[]{:T(512)} %constant.14.clone.1), kind=kCustom, calls=%fused_computation.21 | custom fusion | bytes 524289
  546.7 0.6 reshape.25
  547.4 7.1 fusion.12
  554.5 321.2 %reduce-scatter.2.cloned.1.call-done = f32[8,2048]{1,0:T(8,128)} async-done(((f32[512,2048]{1,0:T(8,128)}), f32[8,2048]{1,0:T(8,128)}) %reduce-scatter.2.cloned.1.call-update) | async-done | bytes 65552 | tf_op jit(solution)/shard_map/reduce_scatter | solution.py:70
  875.7 1.6 fusion.23
  877.3 54.9 %all-reduce = (f32[8]{0:T(128)S(1)}, f32[8]{0:T(128)S(1)}) all-reduce(f32[8]{0:T(128)S(1)} %get-tuple-element.4, f32[8]{0:T(128)S(1)} %get-tuple-element.3), channel_id=1, replica_groups=mesh['dp'=4,'tensor'=16,'rep'=4] {'rep'}, use_global_device_ids=true, to_apply=%region_9.10 | all-reduce | flops 16 | bytes 128 | tf_op jit(solution)/shard_map/psum | solution.py:80
  932.2 0.5 add_divide_fusion
  (36 shorter events, 0.9 us)
Async XLA Ops:
  7.2 53.0 %all-gather.7.cloned.1.call-start = ((), (), s32[]{:S(2)}) async-start(), calls=%async_computation.2 | async-start | bytes 4587520 | tf_op jit(solution)/shard_map/all_gather | solution.py:43
  7.9 100.8 %copy-start = (bf16[128,2048]{1,0:T(8,128)(2,1)S(1)}, bf16[128,2048]{1,0:T(8,128)(2,1)}, u32[]{:S(2)}) copy-start(bf16[128,2048]{1,0:T(8,128)(2,1)} %param.10) | copy-start | bytes 1572868
  7.9 100.8 %copy-start.2 = (f32[2048]{0:T(1024)S(1)}, f32[2048]{0:T(1024)}, u32[]{:S(2)}) copy-start(f32[2048]{0:T(1024)} %param.11) | copy-start | bytes 24580
  7.9 100.8 %all-gather.5.cloned.1.call-start = ((), (), s32[]{:S(2)}) async-start(), calls=%async_computation.1 | async-start | bytes 4587520 | tf_op jit(solution)/shard_map/all_gather | solution.py:38
  8.7 148.6 %all-gather.9.cloned.1.call-start = ((), (), s32[]{:S(2)}) async-start(), calls=%async_computation.3 | async-start | bytes 4587520 | tf_op jit(solution)/shard_map/all_gather | solution.py:50
  9.4 196.4 %all-reduce.10.cloned.1.call-start = ((), (), s32[]{:S(2)}) async-start(), calls=%async_computation.8 | async-start | bytes 1835008 | tf_op jit(solution)/shard_map/psum | solution.py:46
  112.3 246.9 %all-reduce.6.cloned.1.call-start = ((), (), s32[]{:S(2)}) async-start(), calls=%async_computation.4 | async-start | bytes 2097152 | tf_op jit(solution)/shard_map/psum | solution.py:54
  205.8 196.6 %copy-start.3 = (f32[2048]{0:T(1024)S(1)}, f32[2048]{0:T(1024)}, u32[]{:S(2)}) copy-start(f32[2048]{0:T(1024)} %param.18) | copy-start | bytes 24580
  209.9 192.5 %all-gather.11.cloned.1.call-start = ((), (), s32[]{:S(2)}) async-start(), calls=%async_computation.5 | async-start | bytes 2621440 | tf_op jit(solution)/shard_map/all_gather | solution.py:59
  361.4 47.7 %copy-start.1 = (s32[512,64]{0,1:T(8,128)S(1)}, s32[512,64]{0,1:T(8,128)}, u32[]{:S(2)}) copy-start(s32[512,64]{0,1:T(8,128)} %param.19) | copy-start | bytes 393220
  361.4 47.7 %copy-start.5 = (s32[2]{0:T(128)S(1)}, s32[2]{0:T(128)}, u32[]{:S(2)}) copy-start(s32[2]{0:T(128)} %constant.46) | copy-start | bytes 28
  361.4 47.8 %copy-start.4 = (s32[2]{0:T(128)S(1)}, s32[2]{0:T(128)}, u32[]{:S(2)}) copy-start(s32[2]{0:T(128)} %constant.49) | copy-start | bytes 28
  361.4 185.9 %all-reduce.8.cloned.1.call-start = ((), (), s32[]{:S(2)}) async-start(), calls=%async_computation.6 | async-start | bytes 4194304 | tf_op jit(solution)/shard_map/psum | solution.py:63
  408.9 138.4 %copy-start.6 = (f32[1024]{0:T(1024)S(1)}, f32[1024]{0:T(1024)}, u32[]{:S(2)}) copy-start(f32[1024]{0:T(1024)} %param.16) | copy-start | bytes 12292
  409.0 466.7 %reduce-scatter.2.cloned.1.call-start = ((), (), s32[]{:S(2)}) async-start(), calls=%async_computation.7 | async-start | bytes 4259840 | tf_op jit(solution)/shard_map/reduce_scatter | solution.py:70
Sparse Core Ops, SparseCore 0:
  9.8 50.2 all-gather.6
  61.9 46.7 all-gather.4
  110.5 46.6 all-gather.8
  159.9 45.9 all-reduce.9
  210.0 149.1 all-reduce.5
  361.5 40.8 all-gather.10
  409.1 62.8 all-reduce.7
  554.6 320.9 reduce-scatter.1
where the time goes:
time: 940 us
  waiting for transfers between devices  693 us (74%)
  local copies, waits for them, and re-layouts  138 us (15%)
  blocking collectives  63.2 us (7%)
  matrix products  25 us (3%)
  between operations  14.3 us (2%)
    reduce_scatter x1, waiting for transfers between devices, body(): lax.psum_scatter(jnp.dot(actives, dec_weight, preferred_element_type=jnp....  321 us
    psum x1, waiting for transfers between devices, body(): block_sum = lax.psum(down_terms, 'tensor')  149 us
    unnamed x18, local copies, waits for them, and re-layouts  137 us
    psum x1, blocking collectives, body(): lax.psum((jnp.sum(misfit * misfit, axis=1), jnp.sum(kept_f * kept_f, axis...  54.9 us
    psum x1, waiting for transfers between devices, body(): gate_pre, up_pre = lax.psum((gate_part, up_part), 'rep')  48.5 us
    all_gather x1, waiting for transfers between devices, body(): lax.all_gather(down_weight, 'dp', axis=2, tiled=True)[:, 0, :]  44.9 us
    all_gather x1, waiting for transfers between devices, body(): lax.all_gather(gate_weight, 'dp', axis=1, tiled=True)[0]  44.8 us
    all_gather x1, waiting for transfers between devices, body(): lax.all_gather(up_weight, 'dp', axis=1, tiled=True)[0]  41.2 us
  transfers between devices with their start and end apart: 8, of which 7 were waited for; matrix products, arithmetic and copies ran while one was open for 16% of the time, Pallas kernels for 0%

commit v1 on v0

--- a/solution.py
+++ b/solution.py
@@ -51,7 +51,7 @@
         preferred_element_type=jnp.float32,
     )
     rows_dev = tok_grp // n_tensor
-    block_sum = lax.psum(down_terms, "tensor")
+    block_sum = jnp.sum(lax.all_gather(down_terms, "tensor"), axis=0)
     group_out = (resid_f + block_sum).astype(jnp.bfloat16)
     resid_rows = lax.dynamic_slice_in_dim(
         group_out, lax.axis_index("tensor") * rows_dev, rows_dev, 0

time: 940 us -> 1010 us (1.074)
  waiting for transfers between devices: 693 us -> 759 us
    all_gather x0 -> x1, waiting for transfers between devices: none -> 225 us  [body(): block_sum = jnp.sum(lax.all_gather(down_terms, 'tensor'), axis=0)]
    psum x1 -> x0, waiting for transfers between devices: 149 us -> none  [body(): block_sum = lax.psum(down_terms, 'tensor')]
    all_gather x1, waiting for transfers between devices: 41 us -> 30.7 us  [body(): slab_input = lax.all_gather(group_out, 'dp', axis=0, tiled=True)]
  transfers between devices with their start and end apart: 8 -> 8, of which waited for: 7 -> 7; matrix products, arithmetic and copies ran while one was open for 16% -> 15% of each run, Pallas kernels for 0% -> 0%
where the time goes in v1:
time: 1010 us
  waiting for transfers between devices  759 us (75%)
  local copies, waits for them, and re-layouts  138 us (14%)
  blocking collectives  62.7 us (6%)
  matrix products  25 us (2%)
  between operations  14.3 us (1%)
  other arithmetic  12 us (1%)
    reduce_scatter x1, waiting for transfers between devices, body(): lax.psum_scatter(jnp.dot(actives, dec_weight, preferred_element_type=jnp....  321 us
    all_gather x1, waiting for transfers between devices, body(): block_sum = jnp.sum(lax.all_gather(down_terms, 'tensor'), axis=0)  225 us
    unnamed x18, local copies, waits for them, and re-layouts  137 us
    psum x1, blocking collectives, body(): lax.psum((jnp.sum(misfit * misfit, axis=1), jnp.sum(kept_f * kept_f, axis...  54.5 us
    psum x1, waiting for transfers between devices, body(): gate_pre, up_pre = lax.psum((gate_part, up_part), 'rep')  48.5 us
    all_gather x1, waiting for transfers between devices, body(): lax.all_gather(down_weight, 'dp', axis=2, tiled=True)[:, 0, :]  44.9 us
    all_gather x1, waiting for transfers between devices, body(): lax.all_gather(gate_weight, 'dp', axis=1, tiled=True)[0]  44.8 us
    all_gather x1, waiting for transfers between devices, body(): lax.all_gather(up_weight, 'dp', axis=1, tiled=True)[0]  41.2 us
  transfers between devices with their start and end apart: 8, of which 7 were waited for; matrix products, arithmetic and copies ran while one was open for 15% of the time, Pallas kernels for 0%

profile of v1, /device:TPU:1, one launch (start us, length us, event | category | flops | bytes accessed | tf_op | source)
XLA Modules:
  0.0 1011.4 jit_solution(12396595572561924730)
XLA Ops:
  7.2 0.7 all-gather.9.cloned.1.call-update
  8.0 0.7 all-gather.7.cloned.1.call-update
  8.7 0.7 all-gather.11.cloned.1.call-update
  9.5 1.2 fusion.8
  10.7 8.3 psum.42
  18.9 41.2 %all-gather.9.cloned.1.call-done = bf16[1,2048,896]{2,1,0:T(8,128)(2,1)} async-done(((bf16[1,512,896]{2,1,0:T(8,128)(2,1)}), bf16[1,2048,896]{2,1,0:T(8,128)(2,1)}) %all-gather.9.cloned.1.call-update) | async-done | bytes 3670032 | tf_op jit(solution)/shard_map/all_gather | solution.py:43
  60.1 3.8 fusion.2
  63.9 44.8 %all-gather.7.cloned.1.call-done = bf16[1,2048,896]{2,1,0:T(8,128)(2,1)} async-done(((bf16[1,512,896]{2,1,0:T(8,128)(2,1)}), bf16[1,2048,896]{2,1,0:T(8,128)(2,1)}) %all-gather.7.cloned.1.call-update) | async-done | bytes 3670032 | tf_op jit(solution)/shard_map/all_gather | solution.py:38
  108.7 3.6 fusion.4
  112.4 44.9 %all-gather.11.cloned.1.call-done = bf16[896,1,2048]{2,0,1:T(8,128)(2,1)} async-done(((bf16[896,1,512]{2,0,1:T(8,128)(2,1)}), bf16[896,1,2048]{2,0,1:T(8,128)(2,1)}) %all-gather.11.cloned.1.call-update) | async-done | bytes 3670032 | tf_op jit(solution)/shard_map/all_gather | solution.py:50
  157.3 48.5 %all-reduce.7.cloned.1.call-done = (f32[128,896]{1,0:T(8,128)}, f32[128,896]{1,0:T(8,128)}) async-done(((f32[128,896]{1,0:T(8,128)}, f32[128,896]{1,0:T(8,128)}), (f32[128,896]{1,0:T(8,128)}, f32[128,896]{1,0:T(8,128)})) %all-reduce.7.cloned.1.call-update) | async-done | bytes 917520 | tf_op jit(solution)/shard_map/psum | solution.py:46
  205.8 4.1 fusion
  210.0 225.4 %all-gather.15.cloned.1.call-done = f32[2048,2048]{1,0:T(8,128)} async-done(((f32[128,2048]{1,0:T(8,128)}), f32[2048,2048]{1,0:T(8,128)}) %all-gather.15.cloned.1.call-update) | async-done | bytes 16777232 | tf_op jit(solution)/shard_map/all_gather | solution.py:54
  435.4 7.4 reduce_sum.37
  442.9 0.9 fusion.11
  443.9 30.7 %all-gather.13.cloned.1.call-done = bf16[512,2048]{1,0:T(8,128)(2,1)} async-done(((bf16[128,2048]{1,0:T(8,128)(2,1)}), bf16[512,2048]{1,0:T(8,128)(2,1)}) %all-gather.13.cloned.1.call-update) | async-done | bytes 2097168 | tf_op jit(solution)/shard_map/all_gather | solution.py:59
  474.6 6.5 fusion.6
  481.8 137.1 %scatter_custom_fusion = pred[524288]{0:T(1024)(128)(4,1)S(1)} fusion(s32[32768]{0:T(1024)S(1)} %reshape.26, pred[32768]{0:T(1024)(128)(4,1)S(1)} %broadcast.49, pred[]{:T(512)} %constant.14.clone.1), kind=kCustom, calls=%fused_computation.21 | custom fusion | bytes 524289
  618.9 0.6 reshape.25
  619.6 7.1 fusion.12
  626.7 321.2 %reduce-scatter.2.cloned.1.call-done = f32[8,2048]{1,0:T(8,128)} async-done(((f32[512,2048]{1,0:T(8,128)}), f32[8,2048]{1,0:T(8,128)}) %reduce-scatter.2.cloned.1.call-update) | async-done | bytes 65552 | tf_op jit(solution)/shard_map/reduce_scatter | solution.py:70
  947.9 1.6 fusion.23
  949.5 54.5 %all-reduce = (f32[8]{0:T(128)S(1)}, f32[8]{0:T(128)S(1)}) all-reduce(f32[8]{0:T(128)S(1)} %get-tuple-element.4, f32[8]{0:T(128)S(1)} %get-tuple-element.3), channel_id=1, replica_groups=mesh['dp'=4,'tensor'=16,'rep'=4] {'rep'}, use_global_device_ids=true, to_apply=%region_9.10 | all-reduce | flops 16 | bytes 128 | tf_op jit(solution)/shard_map/psum | solution.py:80
  1004.0 0.5 add_divide_fusion
  (37 shorter events, 1.0 us)
Async XLA Ops:
  7.2 53.0 %all-gather.9.cloned.1.call-start = ((), (), s32[]{:S(2)}) async-start(), calls=%async_computation.2 | async-start | bytes 4587520 | tf_op jit(solution)/shard_map/all_gather | solution.py:43
  7.9 100.8 %copy-start = (bf16[128,2048]{1,0:T(8,128)(2,1)S(1)}, bf16[128,2048]{1,0:T(8,128)(2,1)}, u32[]{:S(2)}) copy-start(bf16[128,2048]{1,0:T(8,128)(2,1)} %param.10) | copy-start | bytes 1572868
  7.9 100.8 %copy-start.2 = (f32[2048]{0:T(1024)S(1)}, f32[2048]{0:T(1024)}, u32[]{:S(2)}) copy-start(f32[2048]{0:T(1024)} %param.11) | copy-start | bytes 24580
  7.9 100.8 %all-gather.7.cloned.1.call-start = ((), (), s32[]{:S(2)}) async-start(), calls=%async_computation.1 | async-start | bytes 4587520 | tf_op jit(solution)/shard_map/all_gather | solution.py:38
  8.7 148.6 %all-gather.11.cloned.1.call-start = ((), (), s32[]{:S(2)}) async-start(), calls=%async_computation.3 | async-start | bytes 4587520 | tf_op jit(solution)/shard_map/all_gather | solution.py:50
  9.4 196.4 %all-reduce.7.cloned.1.call-start = ((), (), s32[]{:S(2)}) async-start(), calls=%async_computation.8 | async-start | bytes 1835008 | tf_op jit(solution)/shard_map/psum | solution.py:46
  112.3 323.1 %all-gather.15.cloned.1.call-start = ((), (), s32[]{:S(2)}) async-start(), calls=%async_computation.7 | async-start | bytes 17825792 | tf_op jit(solution)/shard_map/all_gather | solution.py:54
  209.9 264.7 %all-gather.13.cloned.1.call-start = ((), (), s32[]{:S(2)}) async-start(), calls=%async_computation.4 | async-start | bytes 2621440 | tf_op jit(solution)/shard_map/all_gather | solution.py:59
  435.4 39.2 %copy-start.3 = (f32[2048]{0:T(1024)S(1)}, f32[2048]{0:T(1024)}, u32[]{:S(2)}) copy-start(f32[2048]{0:T(1024)} %param.18) | copy-start | bytes 24580
  443.8 37.4 %copy-start.1 = (s32[512,64]{0,1:T(8,128)S(1)}, s32[512,64]{0,1:T(8,128)}, u32[]{:S(2)}) copy-start(s32[512,64]{0,1:T(8,128)} %param.19) | copy-start | bytes 393220
  443.8 37.5 %copy-start.5 = (s32[2]{0:T(128)S(1)}, s32[2]{0:T(128)}, u32[]{:S(2)}) copy-start(s32[2]{0:T(128)} %constant.46) | copy-start | bytes 28
  443.8 37.6 %copy-start.4 = (s32[2]{0:T(128)S(1)}, s32[2]{0:T(128)}, u32[]{:S(2)}) copy-start(s32[2]{0:T(128)} %constant.49) | copy-start | bytes 28
  443.8 175.7 %all-reduce.5.cloned.1.call-start = ((), (), s32[]{:S(2)}) async-start(), calls=%async_computation.5 | async-start | bytes 4194304 | tf_op jit(solution)/shard_map/psum | solution.py:63
  481.1 138.4 %copy-start.6 = (f32[1024]{0:T(1024)S(1)}, f32[1024]{0:T(1024)}, u32[]{:S(2)}) copy-start(f32[1024]{0:T(1024)} %param.16) | copy-start | bytes 12292
  481.2 466.7 %reduce-scatter.2.cloned.1.call-start = ((), (), s32[]{:S(2)}) async-start(), calls=%async_computation.6 | async-start | bytes 4259840 | tf_op jit(solution)/shard_map/reduce_scatter | solution.py:70
Sparse Core Ops, SparseCore 0:
  9.8 50.2 all-gather.8
  61.9 46.7 all-gather.6
  110.5 46.6 all-gather.10
  159.9 45.9 all-reduce.6
  210.0 225.3 all-gather.14
  443.9 30.6 all-gather.12
  481.3 62.8 all-reduce.4
  626.8 321.0 reduce-scatter.1
